TPU v7x, 256 devices: a whole 4x4x8 slice. The times are simulated.
256 devices in a mesh: seq: 16 (over y, z_lo, core), head: 16 (over z_hi, x).
Axes of the slice: x: 4, y: 4, z: 8 (z_hi: 4, z_lo: 2; z = z_hi * 2 + z_lo), core: 2. Of those that a mesh axis runs over, the one named last changes fastest.
Arguments:
- query_latent: bfloat16 [4096, 128, 576], P('seq', 'head'), may hold values from -6 to 6
- key_latent: bfloat16 [2048, 576], P('seq'), may hold values from -6 to 6
- normalizer: float32 [4096, 128], P('seq', 'head'), may hold values from 7 to 9
- index_query: bfloat16 [4096, 64, 128], P('seq', 'head'), may hold values from -20 to 20
- index_key: bfloat16 [2048, 128], P('seq'), may hold values from -6.5 to 6.5
- index_weight: float32 [4096, 64], P('seq', 'head'), may hold values from 0.05 to 0.5
- kept: int32 [32, 16], P('seq'), may hold values from 0 to 1, as said below
Outputs:
- index_query_grad: bfloat16 [4096, 64, 128], P('seq', 'head')
- index_key_grad: float32 [2048, 128], P('seq')
Inputs may be any that keep to these rules, and one draw needn't show every extreme that they name: `kept`: every query tile keeps the key tile whose position matches its own block of 256 queries.
All inputs are finite; a program needn't handle non-finite values.
Results may differ from a plain program's by a relative error of at most 0.009.
Values may be sent and summed in bfloat16 or wider, within the bound.
No kernel may reach another device: no remote copies, remote signals or barrier semaphores. Data moves between devices by JAX's collectives and lax.ppermute only.
A program may use at most 64 MiB of HBM per device.

v0:
```python
import jax
import jax.numpy as jnp
from jax import lax
from jax.sharding import PartitionSpec as P

attn_scale = 192.0 ** (-0.5)


def joined_along(tiles, dim):
    dims = list(tiles.shape[1:])
    dims[dim] *= tiles.shape[0]
    return jnp.moveaxis(tiles, 0, dim).reshape(dims)


def from_everyone(value, axis):
    copies = jnp.broadcast_to(value, (lax.axis_size(axis), *value.shape))
    return lax.all_to_all(copies, axis, split_axis=0, concat_axis=0, tiled=True)


def gathered_copies(value, axis, dim):
    return joined_along(from_everyone(value, axis), dim)


def sent_together(arrays, axis, dim, along):
    widths = [a.shape[along] for a in arrays]
    both = jnp.concatenate(arrays, axis=along)
    out = lax.psum_scatter(both, axis, scatter_dimension=dim, tiled=True)
    return tuple(jnp.split(out, [sum(widths[:k]) for k in range(1, len(widths))], axis=along))


def cut_along(value, dim, count):
    before, after = (value.shape[:dim], value.shape[dim + 1 :])
    return jnp.moveaxis(value.reshape(*before, count, -1, *after), dim, 0)


def sent_and_summed(value, axis, dim):
    count = lax.axis_size(axis)
    tiles = lax.all_to_all(cut_along(value, dim, count), axis, 0, 0, tiled=True)
    return jnp.sum(tiles.astype(jnp.float32), axis=0)


def of_everyone(value, axis):
    return from_everyone(value, axis).astype(jnp.float32).sum(axis=0)


def logit_gradient(head_sum, logit, keep):
    target = head_sum / jnp.sum(head_sum, axis=1, keepdims=True)
    top = jnp.max(jnp.where(keep, logit, -jnp.inf), axis=1, keepdims=True)
    expo = jnp.where(keep, jnp.exp(jnp.where(keep, logit, top) - top), 0.0)
    return expo / jnp.sum(expo, axis=1, keepdims=True) - target


def local(query_latent, key_latent, normalizer, index_query, index_key, index_weight, kept):
    query_rows, head_count, width = query_latent.shape
    tile_rows = index_key.shape[0]
    index_scale = index_query.shape[2] ** (-0.5)
    keys_whole = gathered_copies(index_key, "seq", 0)
    allow = jnp.repeat(jnp.repeat(kept, tile_rows, axis=0), tile_rows, axis=1) > 0
    z_val = (
        jnp.einsum("tjd,sd->tjs", index_query, keys_whole, preferred_element_type=jnp.float32)
        * index_scale
    )
    logit_part = jnp.sum(index_weight[:, :, None] * jnp.maximum(z_val, 0.0), axis=1)
    flat_query = query_latent.reshape(query_rows * head_count, width)
    piece = lax.all_gather(key_latent, "seq", axis=0, tiled=True)
    count = piece.shape[0]
    scores = (
        jnp.einsum("rc,sc->rs", flat_query, piece, preferred_element_type=jnp.float32) * attn_scale
    )
    prob = jnp.exp(scores.reshape(query_rows, head_count, count) - normalizer[:, :, None])
    partial_value = jnp.where(allow, jnp.sum(prob, axis=1), 0.0)
    head_sum, logit = sent_together((partial_value, logit_part), "head", 0, 1)
    share = head_sum.shape[0]
    begin = lax.axis_index("head") * share
    keep_share = lax.dynamic_slice_in_dim(allow, begin, share, 0)
    gradient = lax.all_gather(
        logit_gradient(head_sum, logit, keep_share), "head", axis=0, tiled=True
    )
    dz_val = jnp.where(z_val > 0, gradient[:, None, :] * index_weight[:, :, None], 0.0).astype(
        jnp.bfloat16
    )
    dquery = (
        jnp.einsum("tjs,sd->tjd", dz_val, keys_whole, preferred_element_type=jnp.float32)
        * index_scale
    ).astype(jnp.bfloat16)
    dkey = sent_and_summed(
        (
            jnp.einsum("tjs,tjd->sd", dz_val, index_query, preferred_element_type=jnp.float32)
            * index_scale
        ).astype(jnp.bfloat16),
        "seq",
        0,
    )
    dkey = of_everyone(dkey.astype(jnp.bfloat16), "head").astype(jnp.float32)
    return (dquery, dkey)


def solution(mesh):
    return jax.shard_map(
        local,
        mesh=mesh,
        in_specs=(
            P("seq", "head", None),
            P("seq", None),
            P("seq", "head"),
            P("seq", "head", None),
            P("seq", None),
            P("seq", "head"),
            P("seq", None),
        ),
        out_specs=(P("seq", "head", None), P("seq", None)),
        check_vma=False,
    )
```

profile of v0, /device:TPU:32, one launch (start us, length us, event | category | flops | bytes accessed | tf_op | source)
XLA Modules:
  0.0 279.0 jit_solution(5726327886860402368)
XLA Ops:
  7.2 0.0 all-gather.3.cloned.1.call-start
  7.2 0.7 all-gather.3.cloned.1.call-update
  7.9 1.6 broadcast_in_dim.40
  9.5 5.9 %all-to-all-start = ((bf16[16,128,128]{2,1,0:T(8,128)(2,1)}), bf16[16,128,128]{2,1,0:T(8,128)(2,1)S(1)}, u32[]{:S(2)}, u32[]{:S(2)}) async-start(bf16[16,128,128]{2,1,0:T(8,128)(2,1)} %broadcast_in_dim.40), calls=%async_computation | async-start | bytes 1048576 | tf_op jit(solution)/shard_map/all_to_all | solution.py:17
  15.5 0.0 reduce-scatter.2.cloned.1.call-start
  15.5 0.8 copy.22
  16.4 4.9 %copy.21 = bf16[256,8,576]{2,1,0:T(8,128)(2,1)} copy(bf16[256,8,576]{0,2,1:T(8,128)(2,1)} %param.7) | data formatting | bytes 4718592 | tf_op args[0]
  21.3 0.7 broadcast_compare_fusion
  22.0 3.2 %all-to-all-done = bf16[16,128,128]{2,1,0:T(8,128)(2,1)S(1)} async-done(((bf16[16,128,128]{2,1,0:T(8,128)(2,1)}), bf16[16,128,128]{2,1,0:T(8,128)(2,1)S(1)}, u32[]{:S(2)}, u32[]{:S(2)}) %all-to-all-start) | async-done | bytes 524320 | tf_op jit(solution)/shard_map/all_to_all | solution.py:17
  25.2 5.8 %multiply_reduce_fusion = (f32[256,2048]{1,0:T(8,128)S(1)}, f32[256,4,2048]{2,0,1:T(8,128)}) fusion(f32[256,4]{0,1:T(4,128)} %param.12, bf16[2048,128,1]{1,0,2:T(8,128)(2,1)S(1)} %bitcast.31, bf16[256,4,128]{2,1,0:T(4,128)(2,1)} %param.10), kind=kOutput, calls=%fused_computation.6 | convolution fusion | flops 544735232 | bytes 11276288 | tf_op jit(solution)/shard_map/tjd,sd->tjs/dot_general | solution.py:60
  31.0 21.6 %all-gather.3.cloned.1.call-done = bf16[2048,576]{0,1:T(8,128)(2,1)} async-done(((bf16[128,576]{0,1:T(8,128)(2,1)}), bf16[2048,576]{0,1:T(8,128)(2,1)}) %all-gather.3.cloned.1.call-update) | async-done | bytes 2359312 | tf_op jit(solution)/shard_map/all_gather | solution.py:65
  52.6 13.1 %fusion.1 = f32[256,2048]{1,0:T(8,128)S(1)} fusion(bf16[2048,576]{0,1:T(8,128)(2,1)} %all-gather.3.cloned.1.call-done, f32[256,8]{1,0:T(8,128)S(1)} %copy.22, bf16[256,8,576]{2,1,0:T(8,128)(2,1)} %copy.21), kind=kOutput, calls=%fused_computation.2 | convolution fusion | flops 4843896832 | bytes 6823936 | tf_op jit(solution)/shard_map/rc,sc->rs/dot_general | solution.py:68
  65.7 1.3 broadcast_in_dim.42
  67.0 0.4 broadcast_select_fusion
  67.4 2.4 pad_maximum_fusion
  69.8 0.2 all-gather.5.cloned.1.call-start
  70.0 0.3 copy.37
  70.3 95.6 %reduce-scatter.2.cloned.1.call-done = f32[16,4096]{1,0:T(8,128)} async-done(((f32[256,4096]{1,0:T(8,128)}), f32[16,4096]{1,0:T(8,128)}) %reduce-scatter.2.cloned.1.call-update) | async-done | bytes 262160 | tf_op jit(solution)/shard_map/reduce_scatter | solution.py:27
  165.9 1.0 select_reduce_fusion
  167.0 1.2 fusion.24
  168.1 1.7 divide_subtract_fusion
  169.9 4.8 %fusion.16 = u8[256,2048]{1,0:T(8,128)(4,1)S(1)} fusion(f32[256,4,2048]{2,0,1:T(8,128)} %get-tuple-element.11), kind=kLoop, calls=%fused_computation.22 | loop fusion | flops 12058624 | bytes 8912896
  174.7 52.6 %all-gather.5.cloned.1.call-done = f32[256,2048]{1,0:T(8,128)} async-done(((f32[16,2048]{1,0:T(8,128)}), f32[256,2048]{1,0:T(8,128)}) %all-gather.5.cloned.1.call-update) | async-done | bytes 2097168 | tf_op jit(solution)/shard_map/all_gather | solution.py:76
  227.3 3.6 %fusion.15 = bf16[2048,128]{1,0:T(8,128)(2,1)S(1)} fusion(f32[256,2048]{1,0:T(8,128)} %all-gather.5.cloned.1.call-done, f32[256,4]{0,1:T(4,128)S(1)} %copy-done.1, u8[256,2048]{1,0:T(8,128)(4,1)S(1)} %fusion.16, bf16[256,4,128]{2,1,0:T(4,128)(2,1)S(1)} %copy-done), kind=kOutput, calls=%fused_computation.21 | convolution fusion | flops 552075264 | bytes 3411968 | tf_op jit(solution)/shard_map/tjs,tjd->sd/dot_general | solution.py:88
  231.0 15.3 %all_to_all.15 = bf16[16,128,128]{2,1,0:T(8,128)(2,1)S(1)} all-to-all(bf16[16,128,128]{2,1,0:T(8,128)(2,1)S(1)} %bitcast.36), channel_id=1, replica_groups=mesh['seq'=16,'head'=16] {'seq'}, dimensions={0} | all-to-all | bytes 1048576 | tf_op jit(solution)/shard_map/all_to_all | solution.py:38
  246.2 0.1 reduce_sum.61
  246.3 0.9 broadcast_in_dim.47
  247.2 6.2 %all-to-all-start.2 = ((bf16[16,128,128]{2,1,0:T(8,128)(2,1)}), bf16[16,128,128]{2,1,0:T(8,128)(2,1)S(1)}, u32[]{:S(2)}, u32[]{:S(2)}) async-start(bf16[16,128,128]{2,1,0:T(8,128)(2,1)} %broadcast_in_dim.47), calls=%async_computation.3 | async-start | bytes 1048576 | tf_op jit(solution)/shard_map/all_to_all | solution.py:17
  253.4 3.1 %fusion.18 = bf16[256,4,128]{2,0,1:T(8,128)(2,1)S(1)} fusion(bf16[2048,128,1]{1,0,2:T(8,128)(2,1)S(1)} %bitcast.32, f32[256,2048]{1,0:T(8,128)} %all-gather.5.cloned.1.call-done, f32[256,4]{0,1:T(4,128)S(1)} %copy-done.1, u8[256,2048]{1,0:T(8,128)(4,1)S(1)} %fusion.16), kind=kOutput, calls=%fused_computation.25 | convolution fusion | flops 551813120 | bytes 3411968 | tf_op jit(solution)/shard_map/tjs,sd->tjd/dot_general | solution.py:83
  256.6 0.9 copy.25
  257.5 14.3 %all-to-all-done.2 = bf16[16,128,128]{2,1,0:T(8,128)(2,1)S(1)} async-done(((bf16[16,128,128]{2,1,0:T(8,128)(2,1)}), bf16[16,128,128]{2,1,0:T(8,128)(2,1)S(1)}, u32[]{:S(2)}, u32[]{:S(2)}) %all-to-all-start.2) | async-done | bytes 524320 | tf_op jit(solution)/shard_map/all_to_all | solution.py:17
  271.8 0.7 convert_reduce_fusion
  (7 shorter events, 0.1 us)
Async XLA Ops:
  7.2 45.5 %all-gather.3.cloned.1.call-start = ((), (), s32[]{:S(2)}) async-start(), calls=%async_computation.4 | async-start | bytes 2506752 | tf_op jit(solution)/shard_map/all_gather | solution.py:65
  9.5 15.6 %all-to-all-start = ((bf16[16,128,128]{2,1,0:T(8,128)(2,1)}), bf16[16,128,128]{2,1,0:T(8,128)(2,1)S(1)}, u32[]{:S(2)}, u32[]{:S(2)}) async-start(bf16[16,128,128]{2,1,0:T(8,128)(2,1)} %broadcast_in_dim.40), calls=%async_computation | async-start | bytes 1048576 | tf_op jit(solution)/shard_map/all_to_all | solution.py:17
  15.5 150.4 %reduce-scatter.2.cloned.1.call-start = ((), (), s32[]{:S(2)}) async-start(), calls=%async_computation.5 | async-start | bytes 4456448 | tf_op jit(solution)/shard_map/reduce_scatter | solution.py:27
  69.7 157.6 %copy-start = (bf16[256,4,128]{2,1,0:T(4,128)(2,1)S(1)}, bf16[256,4,128]{2,1,0:T(4,128)(2,1)}, u32[]{:S(2)}) copy-start(bf16[256,4,128]{2,1,0:T(4,128)(2,1)} %param.10) | copy-start | bytes 786436
  69.7 157.6 %copy-start.1 = (f32[256,4]{0,1:T(4,128)S(1)}, f32[256,4]{0,1:T(4,128)}, u32[]{:S(2)}) copy-start(f32[256,4]{0,1:T(4,128)} %param.12) | copy-start | bytes 12292
  69.8 157.5 %all-gather.5.cloned.1.call-start = ((), (), s32[]{:S(2)}) async-start(), calls=%async_computation.6 | async-start | bytes 2228224 | tf_op jit(solution)/shard_map/all_gather | solution.py:76
  247.2 24.6 %all-to-all-start.2 = ((bf16[16,128,128]{2,1,0:T(8,128)(2,1)}), bf16[16,128,128]{2,1,0:T(8,128)(2,1)S(1)}, u32[]{:S(2)}, u32[]{:S(2)}) async-start(bf16[16,128,128]{2,1,0:T(8,128)(2,1)} %broadcast_in_dim.47), calls=%async_computation.3 | async-start | bytes 1048576 | tf_op jit(solution)/shard_map/all_to_all | solution.py:17
Sparse Core Ops, SparseCore 0:
  9.7 42.8 all-gather.2
  69.9 95.9 reduce-scatter.1
  170.0 57.2 all-gather.4
where the time goes:
time: 280 us; the launch traced here: 279 us
  waiting for transfers between devices  188 us (67%)
  matrix products  25.7 us (9%)
  blocking collectives  15.3 us (5%)
  between operations  13.8 us (5%)
  other arithmetic  13 us (5%)
  starting transfers between devices  12.5 us (4%)
  local copies, waits for them, and re-layouts  10.8 us (4%)
    reduce_scatter x1, waiting for transfers between devices, sent_together(): out = lax.psum_scatter(both, axis, scatter_dimension=dim, tiled=True)  95.6 us
    all_gather x1, waiting for transfers between devices, local(): lax.all_gather(logit_gradient(head_sum, logit, keep_share), 'head', axis=...  52.6 us
    all_gather x1, waiting for transfers between devices, local(): piece = lax.all_gather(key_latent, 'seq', axis=0, tiled=True)  21.6 us
    all_to_all x2, waiting for transfers between devices, from_everyone(): return lax.all_to_all(copies, axis, split_axis=0, concat_axis=0, tiled=True)  17.5 us
    all_to_all x1, blocking collectives, sent_and_summed(): tiles = lax.all_to_all(cut_along(value, dim, count), axis, 0, 0, tiled=True)  15.3 us
    dot_general x1, matrix products, local(): jnp.einsum('rc,sc->rs', flat_query, piece, preferred_element_type=jnp.flo...  13.1 us
    all_to_all x2, starting transfers between devices, from_everyone(): return lax.all_to_all(copies, axis, split_axis=0, concat_axis=0, tiled=True)  12.2 us
    unnamed x8, local copies, waits for them, and re-layouts  6.97 us
  transfers between devices with their start and end apart: 5, of which 5 were waited for; matrix products, arithmetic and copies ran while one was open for 8% of the time, Pallas kernels for 0%

commit v1 on v0

--- a/solution.py
+++ b/solution.py
@@ -62,7 +62,9 @@
     )
     logit_part = jnp.sum(index_weight[:, :, None] * jnp.maximum(z_val, 0.0), axis=1)
     flat_query = query_latent.reshape(query_rows * head_count, width)
-    piece = lax.all_gather(key_latent, "seq", axis=0, tiled=True)
+    piece = jnp.concatenate(
+        lax.all_to_all(jnp.stack([key_latent] * lax.axis_size("seq")), "seq", 0, 0), axis=0
+    )
     count = piece.shape[0]
     scores = (
         jnp.einsum("rc,sc->rs", flat_query, piece, preferred_element_type=jnp.float32) * attn_scale

time: 280 us -> 290 us (1.036)
  blocking collectives: 15.3 us -> 30.8 us
  waiting for transfers between devices: 188 us -> 185 us
    all_gather x1 -> x0, waiting for transfers between devices: 21.6 us -> none  [local(): piece = lax.all_gather(key_latent, 'seq', axis=0, tiled=True)]
    all_to_all x0 -> x1, waiting for transfers between devices: none -> 20.9 us  [local(): lax.all_to_all(jnp.stack([key_latent] * lax.axis_size('seq')), 'seq', 0, 0)]
    all_to_all x0 -> x1, blocking collectives: none -> 15.6 us  [from_everyone(): return lax.all_to_all(copies, axis, split_axis=0, concat_axis=0, tiled=True)]
    all_to_all x2 -> x1, starting transfers between devices: 12.2 us -> 6.23 us  [from_everyone(): return lax.all_to_all(copies, axis, split_axis=0, concat_axis=0, tiled=True)]
    all_to_all x0 -> x1, starting transfers between devices: none -> 5.55 us  [local(): lax.all_to_all(jnp.stack([key_latent] * lax.axis_size('seq')), 'seq', 0, 0)]
    all_to_all x2 -> x1, waiting for transfers between devices: 17.5 us -> 14.3 us  [from_everyone(): return lax.all_to_all(copies, axis, split_axis=0, concat_axis=0, tiled=True)]
    unnamed x8 -> x14, local copies, waits for them, and re-layouts: 6.97 us -> 4.87 us
  transfers between devices with their start and end apart: 5 -> 4, of which waited for: 5 -> 4; matrix products, arithmetic and copies ran while one was open for 8% -> 6% of each run, Pallas kernels for 0% -> 0%
where the time goes in v1:
time: 290 us; the launch traced here: 289 us
  waiting for transfers between devices  185 us (64%)
  blocking collectives  30.8 us (11%)
  matrix products  24.4 us (8%)
  between operations  14.2 us (5%)
  other arithmetic  12.3 us (4%)
  starting transfers between devices  12 us (4%)
  local copies, waits for them, and re-layouts  10.6 us (4%)
    reduce_scatter x1, waiting for transfers between devices, sent_together(): out = lax.psum_scatter(both, axis, scatter_dimension=dim, tiled=True)  96.8 us
    all_gather x1, waiting for transfers between devices, local(): lax.all_gather(logit_gradient(head_sum, logit, keep_share), 'head', axis=...  52.6 us
    all_to_all x1, waiting for transfers between devices, local(): lax.all_to_all(jnp.stack([key_latent] * lax.axis_size('seq')), 'seq', 0, 0)  20.9 us
    all_to_all x1, blocking collectives, from_everyone(): return lax.all_to_all(copies, axis, split_axis=0, concat_axis=0, tiled=True)  15.6 us
    all_to_all x1, blocking collectives, sent_and_summed(): tiles = lax.all_to_all(cut_along(value, dim, count), axis, 0, 0, tiled=True)  15.3 us
    all_to_all x1, waiting for transfers between devices, from_everyone(): return lax.all_to_all(copies, axis, split_axis=0, concat_axis=0, tiled=True)  14.3 us
    dot_general x1, matrix products, local(): jnp.einsum('rc,sc->rs', flat_query, piece, preferred_element_type=jnp.flo...  12.7 us
    all_to_all x1, starting transfers between devices, from_everyone(): return lax.all_to_all(copies, axis, split_axis=0, concat_axis=0, tiled=True)  6.23 us
  transfers between devices with their start and end apart: 4, of which 4 were waited for; matrix products, arithmetic and copies ran while one was open for 6% of the time, Pallas kernels for 0%

profile of v1, /device:TPU:32, one launch (start us, length us, event | category | flops | bytes accessed | tf_op | source)
XLA Modules:
  0.0 289.1 jit_solution(5512112382199118184)
XLA Ops:
  7.2 0.9 broadcast_in_dim.40
  8.0 15.6 %all_to_all.20 = bf16[16,128,128]{2,1,0:T(8,128)(2,1)S(1)} all-to-all(bf16[16,128,128]{2,1,0:T(8,128)(2,1)S(1)} %broadcast_in_dim.40), channel_id=1, replica_groups=mesh['seq'=16,'head'=16] {'seq'}, dimensions={0} | all-to-all | bytes 1048576 | tf_op jit(solution)/shard_map/all_to_all | solution.py:17
  23.6 2.7 stack.2
  26.4 5.5 %all-to-all-start.1 = ((bf16[16,128,576]{1,2,0:T(8,128)(2,1)}), bf16[16,128,576]{1,2,0:T(8,128)(2,1)}, u32[]{:S(2)}, u32[]{:S(2)}) async-start(bf16[16,128,576]{1,2,0:T(8,128)(2,1)} %stack.2), calls=%async_computation.1 | async-start | bytes 4718592 | tf_op jit(solution)/shard_map/all_to_all | solution.py:66
  31.9 0.0 reduce-scatter.2.cloned.1.call-start
  32.0 0.1 copy.38
  32.1 3.5 %copy.36 = bf16[256,8,576]{2,1,0:T(8,128)(2,1)} copy(bf16[256,8,576]{0,2,1:T(8,128)(2,1)S(1)} %copy-done) | data formatting | bytes 4718592 | tf_op args[0]
  35.6 4.9 %multiply_reduce_fusion = (f32[256,2048]{1,0:T(8,128)S(1)}, f32[256,4,2048]{2,0,1:T(8,128)}) fusion(f32[256,4]{0,1:T(4,128)S(1)} %copy-done.3, bf16[2048,128,1]{1,0,2:T(8,128)(2,1)S(1)} %bitcast.37, bf16[256,4,128]{2,1,0:T(4,128)(2,1)S(1)} %copy-done.1), kind=kOutput, calls=%fused_computation.6 | convolution fusion | flops 544735232 | bytes 11276288 | tf_op jit(solution)/shard_map/tjd,sd->tjs/dot_general | solution.py:60
  40.5 20.9 %all-to-all-done.1 = bf16[16,128,576]{1,2,0:T(8,128)(2,1)} async-done(((bf16[16,128,576]{1,2,0:T(8,128)(2,1)}), bf16[16,128,576]{1,2,0:T(8,128)(2,1)}, u32[]{:S(2)}, u32[]{:S(2)}) %all-to-all-start.1) | async-done | bytes 2359328 | tf_op jit(solution)/shard_map/all_to_all | solution.py:66
  61.5 12.7 %fusion.1 = f32[256,2048]{1,0:T(8,128)S(1)} fusion(f32[256,8]{1,0:T(8,128)S(1)} %copy.38, bf16[256,8,576]{2,1,0:T(8,128)(2,1)} %copy.36, bf16[16,128,576]{1,2,0:T(8,128)(2,1)} %all-to-all-done.1), kind=kOutput, calls=%fused_computation.2 | convolution fusion | flops 4843896832 | bytes 6823936 | tf_op jit(solution)/shard_map/rc,sc->rs/dot_general | solution.py:70
  74.2 1.3 broadcast_in_dim.42
  75.5 0.4 broadcast_select_fusion
  75.9 2.4 pad_maximum_fusion
  78.2 0.0 reduce-scatter.2.cloned.1.call-update
  78.3 0.2 all-gather.2.cloned.1.call-start
  78.5 0.3 copy.58
  78.8 96.8 %reduce-scatter.2.cloned.1.call-done = f32[16,4096]{1,0:T(8,128)} async-done(((f32[256,4096]{1,0:T(8,128)}), f32[16,4096]{1,0:T(8,128)}) %reduce-scatter.2.cloned.1.call-update) | async-done | bytes 262160 | tf_op jit(solution)/shard_map/reduce_scatter | solution.py:27
  175.6 1.0 select_reduce_fusion
  176.7 1.2 fusion.26
  177.9 1.7 divide_subtract_fusion
  179.6 0.0 all-gather.2.cloned.1.call-update
  179.6 4.8 %fusion.18 = u8[256,2048]{1,0:T(8,128)(4,1)S(1)} fusion(f32[256,4,2048]{2,0,1:T(8,128)} %get-tuple-element.15), kind=kLoop, calls=%fused_computation.24 | loop fusion | flops 12058624 | bytes 8912896
  184.4 52.6 %all-gather.2.cloned.1.call-done = f32[256,2048]{1,0:T(8,128)} async-done(((f32[16,2048]{1,0:T(8,128)}), f32[256,2048]{1,0:T(8,128)}) %all-gather.2.cloned.1.call-update) | async-done | bytes 2097168 | tf_op jit(solution)/shard_map/all_gather | solution.py:78
  237.0 3.6 %fusion.15 = bf16[2048,128]{1,0:T(8,128)(2,1)S(1)} fusion(f32[256,2048]{1,0:T(8,128)} %all-gather.2.cloned.1.call-done, f32[256,4]{0,1:T(4,128)S(1)} %copy-done.3, u8[256,2048]{1,0:T(8,128)(4,1)S(1)} %fusion.18, bf16[256,4,128]{2,1,0:T(4,128)(2,1)S(1)} %copy-done.1), kind=kOutput, calls=%fused_computation.21 | convolution fusion | flops 552075264 | bytes 3411968 | tf_op jit(solution)/shard_map/tjs,tjd->sd/dot_general | solution.py:90
  240.7 15.3 %all_to_all.21 = bf16[16,128,128]{2,1,0:T(8,128)(2,1)S(1)} all-to-all(bf16[16,128,128]{2,1,0:T(8,128)(2,1)S(1)} %bitcast.42), channel_id=1, replica_groups=mesh['seq'=16,'head'=16] {'seq'}, dimensions={0} | all-to-all | bytes 1048576 | tf_op jit(solution)/shard_map/all_to_all | solution.py:38
  255.9 0.1 reduce_sum.61
  256.0 0.9 broadcast_in_dim.47
  256.9 6.2 %all-to-all-start.3 = ((bf16[16,128,128]{2,1,0:T(8,128)(2,1)}), bf16[16,128,128]{2,1,0:T(8,128)(2,1)S(1)}, u32[]{:S(2)}, u32[]{:S(2)}) async-start(bf16[16,128,128]{2,1,0:T(8,128)(2,1)} %broadcast_in_dim.47), calls=%async_computation.4 | async-start | bytes 1048576 | tf_op jit(solution)/shard_map/all_to_all | solution.py:17
  263.2 3.1 %fusion.20 = bf16[256,4,128]{2,0,1:T(8,128)(2,1)S(1)} fusion(bf16[2048,128,1]{1,0,2:T(8,128)(2,1)S(1)} %bitcast.38, f32[256,2048]{1,0:T(8,128)} %all-gather.2.cloned.1.call-done, f32[256,4]{0,1:T(4,128)S(1)} %copy-done.3, u8[256,2048]{1,0:T(8,128)(4,1)S(1)} %fusion.18), kind=kOutput, calls=%fused_computation.27 | convolution fusion | flops 551813120 | bytes 3411968 | tf_op jit(solution)/shard_map/tjs,sd->tjd/dot_general | solution.py:85
  266.3 0.9 copy.41
  267.2 14.3 %all-to-all-done.3 = bf16[16,128,128]{2,1,0:T(8,128)(2,1)S(1)} async-done(((bf16[16,128,128]{2,1,0:T(8,128)(2,1)}), bf16[16,128,128]{2,1,0:T(8,128)(2,1)S(1)}, u32[]{:S(2)}, u32[]{:S(2)}) %all-to-all-start.3) | async-done | bytes 524320 | tf_op jit(solution)/shard_map/all_to_all | solution.py:17
  281.5 0.7 convert_reduce_fusion
  (12 shorter events, 0.0 us)
Async XLA Ops:
  8.0 23.9 %copy-start.2 = (f32[256,8]{0,1:T(8,128)S(1)}, f32[256,8]{0,1:T(8,128)}, u32[]{:S(2)}) copy-start(f32[256,8]{0,1:T(8,128)} %param.9) | copy-start | bytes 24580
  8.0 24.1 %copy-start = (bf16[256,8,576]{0,2,1:T(8,128)(2,1)S(1)}, bf16[256,8,576]{0,2,1:T(8,128)(2,1)}, u32[]{:S(2)}) copy-start(bf16[256,8,576]{0,2,1:T(8,128)(2,1)} %param.7) | copy-start | bytes 7077892
  26.4 9.3 %copy-start.4 = (s32[2,16]{1,0:T(2,128)S(1)}, s32[2,16]{1,0:T(2,128)}, u32[]{:S(2)}) copy-start(s32[2,16]{1,0:T(2,128)} %param.13) | copy-start | bytes 388
  26.4 9.3 %copy-start.1 = (bf16[256,4,128]{2,1,0:T(4,128)(2,1)S(1)}, bf16[256,4,128]{2,1,0:T(4,128)(2,1)}, u32[]{:S(2)}) copy-start(bf16[256,4,128]{2,1,0:T(4,128)(2,1)} %param.10) | copy-start | bytes 786436
  26.4 9.3 %copy-start.3 = (f32[256,4]{0,1:T(4,128)S(1)}, f32[256,4]{0,1:T(4,128)}, u32[]{:S(2)}) copy-start(f32[256,4]{0,1:T(4,128)} %param.12) | copy-start | bytes 12292
  26.4 35.1 %all-to-all-start.1 = ((bf16[16,128,576]{1,2,0:T(8,128)(2,1)}), bf16[16,128,576]{1,2,0:T(8,128)(2,1)}, u32[]{:S(2)}, u32[]{:S(2)}) async-start(bf16[16,128,576]{1,2,0:T(8,128)(2,1)} %stack.2), calls=%async_computation.1 | async-start | bytes 4718592 | tf_op jit(solution)/shard_map/all_to_all | solution.py:66
  31.9 143.7 %reduce-scatter.2.cloned.1.call-start = ((), (), s32[]{:S(2)}) async-start(), calls=%async_computation.5 | async-start | bytes 4456448 | tf_op jit(solution)/shard_map/reduce_scatter | solution.py:27
  78.3 158.8 %all-gather.2.cloned.1.call-start = ((), (), s32[]{:S(2)}) async-start(), calls=%async_computation.6 | async-start | bytes 2228224 | tf_op jit(solution)/shard_map/all_gather | solution.py:78
  256.9 24.6 %all-to-all-start.3 = ((bf16[16,128,128]{2,1,0:T(8,128)(2,1)}), bf16[16,128,128]{2,1,0:T(8,128)(2,1)S(1)}, u32[]{:S(2)}, u32[]{:S(2)}) async-start(bf16[16,128,128]{2,1,0:T(8,128)(2,1)} %broadcast_in_dim.47), calls=%async_computation.4 | async-start | bytes 1048576 | tf_op jit(solution)/shard_map/all_to_all | solution.py:17
Sparse Core Ops, SparseCore 0:
  78.4 97.1 reduce-scatter.1
  179.7 57.2 all-gather.1
